TPU v7x, 128 devices: a whole 4x4x4 slice. The times are simulated.
128 devices in a mesh: ent: 32 (over x_hi, z, y), sec: 4 (over x_lo, core).
Axes of the slice: x: 4 (x_hi: 2, x_lo: 2; x = x_hi * 2 + x_lo), y: 4, z: 4, core: 2. Of those that a mesh axis runs over, the one named last changes fastest.
Arguments:
- features: bfloat16 [4096, 256], P('ent'), may hold values from -6 to 6
- theta: bfloat16 [256, 256], replicated, may hold values from -3 to 3
- section_weight: float32 [65536], P(('ent', 'sec')), may hold values from 0.5 to 2
- pair_rows: int32 [128, 32, 512], P(('ent', 'sec')), may hold values from 0 to 511
- pair_cols: int32 [128, 32, 512], P(('ent', 'sec')), may hold values from 0 to 127
- pair_counts: int32 [128, 32], P(('ent', 'sec')), may hold values from 0 to 512, as said below
- cotangent: bfloat16 [4096, 256], P('ent'), may hold values from -24 to 24
Outputs:
- activated: bfloat16 [4096, 256], P('ent')
- grad_features: bfloat16 [4096, 256], P('ent')
- grad_theta: float32 [256, 256], replicated
- grad_weight: float32 [65536], P(('ent', 'sec'))
Inputs may be any that keep to these rules, and one draw needn't show every extreme that they name: Only the first pair_counts[k, j] slots of shard k and block j are used; some shard uses all 512 slots of some block.
All inputs are finite; a program needn't handle non-finite values.
Results may differ from a plain program's by a relative error of at most 0.0059.
Values may be sent and summed in bfloat16 or wider, within the bound.
A program may use at most 64 MiB of HBM per device.

v0:
```python
import jax
import jax.numpy as jnp
from jax import lax
from jax.sharding import PartitionSpec as P


def hot_table(indices, live_slots, offset, table_width):
    hits = (indices - offset)[:, None] == jnp.arange(table_width, dtype=jnp.int32)[None, :]
    return (hits & live_slots[:, None]).astype(jnp.bfloat16)


def body(features, theta, section_weight, pair_rows, pair_cols, pair_counts, cotangent):
    ent_dev = features.shape[0]
    feature_width = features.shape[1]
    sec_dev = section_weight.shape[0]
    blocks_count = pair_rows.shape[1]
    slot_count = pair_rows.shape[2]
    own_block = lax.axis_index("ent")
    row_lists = pair_rows[0]
    col_lists = pair_cols[0]
    usable = jnp.arange(slot_count, dtype=jnp.int32)[None, :] < pair_counts[0][:, None]
    usable_float = usable.astype(jnp.float32)
    entity_index = jnp.arange(blocks_count, dtype=jnp.int32)[:, None] * ent_dev + col_lists
    local_degree = jax.ops.segment_sum(
        usable_float.reshape(-1), entity_index.reshape(-1), num_segments=blocks_count * ent_dev
    )
    entity_degree = lax.psum(local_degree, ("ent", "sec"))
    own_degree = lax.dynamic_slice_in_dim(entity_degree, own_block * ent_dev, ent_dev)
    entity_scale = lax.rsqrt(1.0 + own_degree)[:, None]
    sec_count = jax.ops.segment_sum(
        usable_float.reshape(-1), row_lists.reshape(-1), num_segments=sec_dev
    )
    section_scale = (section_weight / (1.0 + sec_count))[:, None]

    def entity_fold(running, incoming, start_row):
        row_count = incoming.shape[0]
        span_width = min(row_count, ent_dev)
        block_span = max(row_count // ent_dev, 1)
        offset = start_row

        def add_block(turn_index, accum):
            row_slots = lax.dynamic_index_in_dim(row_lists, turn_index, 0, keepdims=False)
            col_slots = lax.dynamic_index_in_dim(col_lists, turn_index, 0, keepdims=False)
            live_slots = lax.dynamic_index_in_dim(usable, turn_index, 0, keepdims=False)
            values = lax.dynamic_slice_in_dim(incoming, turn_index * span_width, span_width, 0)
            col_hot = hot_table(col_slots, live_slots, offset, span_width)
            row_hot = hot_table(row_slots, live_slots, 0, sec_dev)
            picked = jnp.dot(col_hot, values, preferred_element_type=jnp.float32).astype(
                jnp.bfloat16
            )
            return accum + jnp.einsum(
                "ps,pf->sf", row_hot, picked, preferred_element_type=jnp.float32
            )

        return lax.fori_loop(0, block_span, add_block, running)

    def entity_terms(messages, start_row):
        span_width = min(lax.axis_size("ent") * ent_dev, ent_dev)
        block_span = max(lax.axis_size("ent") * ent_dev // ent_dev, 1)
        offset = start_row

        def block_term(turn_index):
            row_slots = lax.dynamic_index_in_dim(row_lists, turn_index, 0, keepdims=False)
            col_slots = lax.dynamic_index_in_dim(col_lists, turn_index, 0, keepdims=False)
            live_slots = lax.dynamic_index_in_dim(usable, turn_index, 0, keepdims=False)
            row_hot = hot_table(row_slots, live_slots, 0, sec_dev)
            col_hot = hot_table(col_slots, live_slots, offset, span_width)
            picked = jnp.dot(row_hot, messages, preferred_element_type=jnp.float32).astype(
                jnp.bfloat16
            )
            return jnp.einsum("pw,pf->wf", col_hot, picked, preferred_element_type=jnp.float32)

        pieces = lax.map(block_term, jnp.arange(block_span, dtype=jnp.int32))
        return pieces.reshape(block_span * span_width, feature_width)

    def collect(messages):
        partial_sum = lax.psum_scatter(
            entity_terms(messages, jnp.int32(0)), "ent", scatter_dimension=0, tiled=True
        )
        return lax.psum(partial_sum, "sec")

    zero_sections = jnp.zeros((sec_dev, feature_width), jnp.float32)
    projected = jnp.dot(features, theta, preferred_element_type=jnp.float32)
    scaled = (entity_scale * projected).astype(jnp.bfloat16)
    gathered = entity_fold(
        zero_sections, lax.all_gather(scaled, "ent", axis=0, tiled=True), jnp.int32(0)
    )
    messages = (section_scale * gathered).astype(jnp.bfloat16)
    collected = collect(messages)
    preact = entity_scale * collected
    activated = jax.nn.silu(preact).astype(jnp.bfloat16)
    sigmoid_pre = jax.nn.sigmoid(preact)
    grad_pre = cotangent.astype(jnp.float32) * sigmoid_pre * (1.0 + preact * (1.0 - sigmoid_pre))
    back_scaled = (entity_scale * grad_pre).astype(jnp.bfloat16)
    back_gathered = entity_fold(
        zero_sections, lax.all_gather(back_scaled, "ent", axis=0, tiled=True), jnp.int32(0)
    )
    grad_weight = jnp.sum(gathered * back_gathered, axis=1) / (1.0 + sec_count)
    back_messages = (section_scale * back_gathered).astype(jnp.bfloat16)
    back_collected = collect(back_messages)
    grad_proj = (entity_scale * back_collected).astype(jnp.bfloat16)
    grad_features = lax.dot_general(
        grad_proj, theta, (((1,), (1,)), ((), ())), preferred_element_type=jnp.float32
    ).astype(jnp.bfloat16)
    local_theta = lax.dot_general(
        features, grad_proj, (((0,), (0,)), ((), ())), preferred_element_type=jnp.float32
    )
    grad_theta = lax.psum(local_theta, "ent")
    return (activated, grad_features, grad_theta, grad_weight)


def solution(mesh):
    placed = (
        P("ent", None),
        P(),
        P(("ent", "sec")),
        P(("ent", "sec"), None, None),
        P(("ent", "sec"), None, None),
        P(("ent", "sec"), None),
        P("ent", None),
    )
    return jax.shard_map(
        body,
        mesh=mesh,
        in_specs=placed,
        out_specs=(P("ent", None), P("ent", None), P(), P(("ent", "sec"))),
        check_vma=False,
    )
```

profile of v0, /device:TPU:0, one launch (start us, length us, event | category | flops | bytes accessed | tf_op | source)
XLA Modules:
  0.0 1644.0 jit_solution(5554662827985014451)
XLA Ops:
  9.2 113.5 %scatter_custom_fusion = f32[4096]{0:T(1024)S(1)} fusion(s32[16384]{0:T(1024)S(1)} %bitcast.81, f32[16384]{0:T(1024)S(1)} %bitcast.82, f32[]{:T(128)} %constant.131.clone.1), kind=kCustom, calls=%fused_computation.76 | custom fusion | flops 16384 | bytes 16388 | tf_op jit(solution)/shard_map/scatter-add | solution.py:24
  122.6 68.3 %psum.28 = f32[4096]{0:T(1024)S(1)} all-reduce(f32[4096]{0:T(1024)S(1)} %scatter_custom_fusion), channel_id=1, replica_groups=mesh['ent'=32,'sec'=4] {'ent','sec'}, use_global_device_ids=true, to_apply=%region_1.0 | all-reduce | flops 4096 | bytes 32768 | tf_op jit(solution)/shard_map/psum | solution.py:27
  193.5 113.4 %scatter_custom_fusion.1 = f32[512]{0:T(512)S(1)} fusion(s32[16384]{0:T(1024)S(1)} %bitcast.84, f32[16384]{0:T(1024)S(1)} %bitcast.83, f32[]{:T(128)} %constant.137.clone.1), kind=kCustom, calls=%fused_computation.78 | custom fusion | flops 16384 | bytes 2052 | tf_op jit(solution)/shard_map/scatter-add | solution.py:30
  307.7 79.9 %while.50 = (s32[]{:T(128)}, f32[512,256]{1,0:T(8,128)S(1)}, s32[32,512]{1,0:T(8,128)}, pred[32,512]{1,0:T(8,128)(4,1)S(1)}, s32[32,512]{1,0:T(8,128)}, /*index=...) while((s32[]{:T(128)}, f32[512,256]{1,0:T(8,128)S(1)}, ...), condition=%wide.region_4.5_spmd.clone, body=%wide.region_3.4_spmd.clone.sunk | while | flops 168820736 | bytes 1128617 | solution.py:55
  308.4 1.7 convolution_add_fusion.4
  313.4 1.7 convolution_add_fusion.4
  315.9 1.7 convolution_add_fusion.4
  318.4 1.7 convolution_add_fusion.4
  320.9 1.7 convolution_add_fusion.4
  323.4 1.7 convolution_add_fusion.4
  325.9 1.7 convolution_add_fusion.4
  330.9 1.7 convolution_add_fusion.4
  333.4 1.7 convolution_add_fusion.4
  335.9 1.7 convolution_add_fusion.4
  340.9 1.7 convolution_add_fusion.4
  343.4 1.7 convolution_add_fusion.4
  348.4 1.7 convolution_add_fusion.4
  350.9 1.7 convolution_add_fusion.4
  353.4 1.7 convolution_add_fusion.4
  355.9 1.7 convolution_add_fusion.4
  365.9 1.7 convolution_add_fusion.4
  368.4 1.7 convolution_add_fusion.4
  383.4 1.7 convolution_add_fusion.4
  385.9 1.7 convolution_add_fusion.4
  387.7 2.4 broadcast.21.clone
  390.2 144.5 %while.48 = (s32[]{:T(128)}, f32[32,128,256]{2,1,0:T(8,128)}, s32[32]{0:T(128)S(1)}, s32[32,512]{1,0:T(8,128)}, pred[32,512]{1,0:T(8,128)(4,1)S(1)}, /*index=5*/...) while((s32[]{:T(128)}, f32[32,128,256]{2,1,0:T(8,128)}, ...), condition=%wide.region_6.7_spmd, body=%wide.region_5.6_spmd.sunk | while | flops 168558592 | bytes 408219 | solution.py:73
  534.8 188.6 %reduce-scatter.3.cloned.1.call-done = f32[128,256]{1,0:T(8,128)} async-done(((f32[4096,256]{1,0:T(8,128)}), f32[128,256]{1,0:T(8,128)}) %reduce-scatter.3.cloned.1.call-update) | async-done | bytes 131088 | tf_op jit(solution)/shard_map/reduce_scatter | solution.py:77
  723.4 32.8 %all-reduce.4.cloned.1.call-done = f32[128,256]{1,0:T(8,128)} async-done(((f32[128,256]{1,0:T(8,128)}), f32[128,256]{1,0:T(8,128)}) %all-reduce.4.cloned.1.call-update) | async-done | bytes 131088 | tf_op jit(solution)/shard_map/psum | solution.py:80
  756.2 1.7 multiply_convert_fusion.3
  758.0 73.9 %all-gather.5.cloned.1.call-done = bf16[4096,256]{1,0:T(8,128)(2,1)} async-done(((bf16[128,256]{1,0:T(8,128)(2,1)}), bf16[4096,256]{1,0:T(8,128)(2,1)}) %all-gather.5.cloned.1.call-update) | async-done | bytes 2097168 | tf_op jit(solution)/shard_map/all_gather | solution.py:96
  831.9 79.9 %while.51 = (s32[]{:T(128)}, f32[512,256]{1,0:T(8,128)S(1)}, s32[32,512]{1,0:T(8,128)}, pred[32,512]{1,0:T(8,128)(4,1)S(1)}, s32[32,512]{1,0:T(8,128)}, /*index=...) while((s32[]{:T(128)}, f32[512,256]{1,0:T(8,128)S(1)}, ...), condition=%wide.region_10.11_spmd.clone, body=%wide.region_9.10_spmd.clone.sunk | while | flops 168820736 | bytes 1128617 | solution.py:55
  832.6 1.7 convolution_add_fusion.5
  842.6 1.7 convolution_add_fusion.5
  845.1 1.7 convolution_add_fusion.5
  860.1 1.7 convolution_add_fusion.5
  862.6 1.7 convolution_add_fusion.5
  877.6 1.7 convolution_add_fusion.5
  880.1 1.7 convolution_add_fusion.5
  895.1 1.7 convolution_add_fusion.5
  897.6 1.7 convolution_add_fusion.5
  912.0 2.4 broadcast.21
  914.4 144.5 %while.49 = (s32[]{:T(128)}, f32[32,128,256]{2,1,0:T(8,128)}, s32[32]{0:T(128)S(1)}, s32[32,512]{1,0:T(8,128)}, pred[32,512]{1,0:T(8,128)(4,1)S(1)}, /*index=5*/...) while((s32[]{:T(128)}, f32[32,128,256]{2,1,0:T(8,128)}, ...), condition=%wide.region_12.13_spmd, body=%wide.region_11.12_spmd.sunk | while | flops 168558592 | bytes 408219 | solution.py:73
  1059.0 190.6 %reduce-scatter.5.cloned.1.call-done = f32[128,256]{1,0:T(8,128)} async-done(((f32[4096,256]{1,0:T(8,128)}), f32[128,256]{1,0:T(8,128)}) %reduce-scatter.5.cloned.1.call-update) | async-done | bytes 131088 | tf_op jit(solution)/shard_map/reduce_scatter | solution.py:77
  1249.7 32.8 %all-reduce.6.cloned.1.call-done = f32[128,256]{1,0:T(8,128)} async-done(((f32[128,256]{1,0:T(8,128)}), f32[128,256]{1,0:T(8,128)}) %all-reduce.6.cloned.1.call-update) | async-done | bytes 131088 | tf_op jit(solution)/shard_map/psum | solution.py:80
  1282.5 1.9 convolution_bitcast_fusion
  1285.0 1.7 convolution_convert_fusion.4
  1286.8 348.6 %all-reduce.8.cloned.1.call-done = f32[256,256]{0,1:T(8,128)} async-done(((f32[256,256]{0,1:T(8,128)}), f32[256,256]{0,1:T(8,128)}) %all-reduce.8.cloned.1.call-update) | async-done | bytes 262160 | tf_op jit(solution)/shard_map/psum | solution.py:108
  1635.4 1.8 copy.11
  (458 shorter events, 279.9 us)
Async XLA Ops:
  7.2 183.8 %copy-start = (bf16[256,256]{1,0:T(8,128)(2,1)S(1)}, bf16[256,256]{1,0:T(8,128)(2,1)}, u32[]{:S(2)}) copy-start(bf16[256,256]{1,0:T(8,128)(2,1)} %param.16) | copy-start | bytes 393220
  7.2 300.5 %all-gather.3.cloned.1.call-start = ((), (), s32[]{:S(2)}) async-start(), calls=%async_computation.2 | async-start | bytes 2162688 | tf_op jit(solution)/shard_map/all_gather | solution.py:86
  192.6 530.7 %reduce-scatter.3.cloned.1.call-start = ((), (), s32[]{:S(2)}) async-start(), calls=%async_computation.3 | async-start | bytes 4325376 | tf_op jit(solution)/shard_map/reduce_scatter | solution.py:77
  390.1 366.0 %copy-start.2 = (bf16[128,256]{1,0:T(8,128)(2,1)S(1)}, bf16[128,256]{1,0:T(8,128)(2,1)}, u32[]{:S(2)}) copy-start(bf16[128,256]{1,0:T(8,128)(2,1)} %param.21) | copy-start | bytes 196612
  534.7 221.5 %all-reduce.4.cloned.1.call-start = ((), (), s32[]{:S(2)}) async-start(), calls=%async_computation.4 | async-start | bytes 262144 | tf_op jit(solution)/shard_map/psum | solution.py:80
  723.4 108.5 %all-gather.5.cloned.1.call-start = ((), (), s32[]{:S(2)}) async-start(), calls=%async_computation.5 | async-start | bytes 2162688 | tf_op jit(solution)/shard_map/all_gather | solution.py:96
  757.9 491.7 %reduce-scatter.5.cloned.1.call-start = ((), (), s32[]{:S(2)}) async-start(), calls=%async_computation.6 | async-start | bytes 4325376 | tf_op jit(solution)/shard_map/reduce_scatter | solution.py:77
  914.4 368.1 %copy-start.1 = (bf16[128,256]{1,0:T(8,128)(2,1)S(1)}, bf16[128,256]{1,0:T(8,128)(2,1)}, u32[]{:S(2)}) copy-start(bf16[128,256]{1,0:T(8,128)(2,1)} %param.15) | copy-start | bytes 196612
  1059.0 223.6 %all-reduce.6.cloned.1.call-start = ((), (), s32[]{:S(2)}) async-start(), calls=%async_computation.7 | async-start | bytes 262144 | tf_op jit(solution)/shard_map/psum | solution.py:80
  1249.7 385.8 %all-reduce.8.cloned.1.call-start = ((), (), s32[]{:S(2)}) async-start(), calls=%async_computation.8 | async-start | bytes 524288 | tf_op jit(solution)/shard_map/psum | solution.py:108
Sparse Core Ops, SparseCore 0:
  192.7 66.8 all-gather.2
  534.8 188.4 reduce-scatter.2
  725.8 30.3 all-reduce.3
  760.1 71.6 all-gather.4
  1059.1 190.4 reduce-scatter.4
  1252.1 30.3 all-reduce.5
  1285.6 349.7 all-reduce.7
where the time goes:
time: 1670 us; the launch traced here: 1640 us
  waiting for transfers between devices  867 us (52%)
  other arithmetic  231 us (14%)
  matrix products  191 us (11%)
  local copies, waits for them, and re-layouts  145 us (9%)
  loops' own time  126 us (8%)
  blocking collectives  68.3 us (4%)
    reduce_scatter x2, waiting for transfers between devices, collect(): lax.psum_scatter(entity_terms(messages, jnp.int32(0)), 'ent', scatter_dim...  379 us
    psum x1, waiting for transfers between devices, body(): grad_theta = lax.psum(local_theta, 'ent')  349 us
    another operation x2, loops' own time, entity_terms(): pieces = lax.map(block_term, jnp.arange(block_span, dtype=jnp.int32))  125 us
    scatter-add x1, other arithmetic, body(): jax.ops.segment_sum(usable_float.reshape(-1), entity_index.reshape(-1), n...  113 us
    scatter-add x1, other arithmetic, body(): jax.ops.segment_sum(usable_float.reshape(-1), row_lists.reshape(-1), num_...  113 us
    dot_general x64, matrix products, add_block(): jnp.einsum('ps,pf->sf', row_hot, picked, preferred_element_type=jnp.float32)  108 us
    dot_general x64, matrix products, block_term(): jnp.einsum('pw,pf->wf', col_hot, picked, preferred_element_type=jnp.float32)  77.7 us
    all_gather x1, waiting for transfers between devices, body(): lax.all_gather(back_scaled, 'ent', axis=0, tiled=True)  73.9 us
  transfers between devices with their start and end apart: 7, of which 6 were waited for; matrix products, arithmetic and copies ran while one was open for 7% of the time, Pallas kernels for 0%

commit v1 on v0

--- a/solution.py
+++ b/solution.py
@@ -1,7 +1,16 @@
+import functools
 import jax
 import jax.numpy as jnp
 from jax import lax
 from jax.sharding import PartitionSpec as P
+
+
+def trace_copies(q_in, axis_key):
+    small = lax.all_gather(q_in, axis_key).sum(axis=0)
+    return small
+
+
+_post_sections = functools.partial(trace_copies, axis_key="sec")
 
 
 def hot_table(indices, live_slots, offset, table_width):
@@ -77,7 +86,7 @@
         partial_sum = lax.psum_scatter(
             entity_terms(messages, jnp.int32(0)), "ent", scatter_dimension=0, tiled=True
         )
-        return lax.psum(partial_sum, "sec")
+        return _post_sections(partial_sum)
 
     zero_sections = jnp.zeros((sec_dev, feature_width), jnp.float32)
     projected = jnp.dot(features, theta, preferred_element_type=jnp.float32)

time: 1670 us -> 1600 us (0.958)
  waiting for transfers between devices: 867 us -> 788 us
    psum x2 -> x0, waiting for transfers between devices: 65.6 us -> none  [collect(): return lax.psum(partial_sum, 'sec')]
  transfers between devices with their start and end apart: 7 -> 5, of which waited for: 6 -> 4; matrix products, arithmetic and copies ran while one was open for 7% -> 7% of each run, Pallas kernels for 0% -> 0%
where the time goes in v1:
time: 1600 us; the launch traced here: 1570 us
  waiting for transfers between devices  788 us (49%)
  other arithmetic  230 us (14%)
  matrix products  190 us (12%)
  local copies, waits for them, and re-layouts  145 us (9%)
  loops' own time  126 us (8%)
  blocking collectives  81.7 us (5%)
    reduce_scatter x2, waiting for transfers between devices, collect(): lax.psum_scatter(entity_terms(messages, jnp.int32(0)), 'ent', scatter_dim...  379 us
    psum x1, waiting for transfers between devices, body(): grad_theta = lax.psum(local_theta, 'ent')  342 us
    another operation x2, loops' own time, entity_terms(): pieces = lax.map(block_term, jnp.arange(block_span, dtype=jnp.int32))  125 us
    scatter-add x1, other arithmetic, body(): jax.ops.segment_sum(usable_float.reshape(-1), entity_index.reshape(-1), n...  113 us
    scatter-add x1, other arithmetic, body(): jax.ops.segment_sum(usable_float.reshape(-1), row_lists.reshape(-1), num_...  113 us
    dot_general x64, matrix products, add_block(): jnp.einsum('ps,pf->sf', row_hot, picked, preferred_element_type=jnp.float32)  108 us
    dot_general x64, matrix products, block_term(): jnp.einsum('pw,pf->wf', col_hot, picked, preferred_element_type=jnp.float32)  77.7 us
    psum x1, blocking collectives, body(): entity_degree = lax.psum(local_degree, ('ent', 'sec'))  68.3 us
  transfers between devices with their start and end apart: 5, of which 4 were waited for; matrix products, arithmetic and copies ran while one was open for 7% of the time, Pallas kernels for 0%

profile of v1, /device:TPU:0, one launch (start us, length us, event | category | flops | bytes accessed | tf_op | source)
XLA Modules:
  0.0 1574.7 jit_solution(8055403188114879739)
XLA Ops:
  9.2 113.5 %scatter_custom_fusion = f32[4096]{0:T(1024)S(1)} fusion(s32[16384]{0:T(1024)S(1)} %bitcast.85, f32[16384]{0:T(1024)S(1)} %bitcast.86, f32[]{:T(128)} %constant.131.clone.1), kind=kCustom, calls=%fused_computation.76 | custom fusion | flops 16384 | bytes 16388 | tf_op jit(solution)/shard_map/scatter-add | solution.py:33
  122.6 68.3 %psum.14 = f32[4096]{0:T(1024)S(1)} all-reduce(f32[4096]{0:T(1024)S(1)} %scatter_custom_fusion), channel_id=1, replica_groups=mesh['ent'=32,'sec'=4] {'ent','sec'}, use_global_device_ids=true, to_apply=%region_1.0 | all-reduce | flops 4096 | bytes 32768 | tf_op jit(solution)/shard_map/psum | solution.py:36
  193.5 113.4 %scatter_custom_fusion.1 = f32[512]{0:T(512)S(1)} fusion(s32[16384]{0:T(1024)S(1)} %bitcast.88, f32[16384]{0:T(1024)S(1)} %bitcast.87, f32[]{:T(128)} %constant.137.clone.1), kind=kCustom, calls=%fused_computation.78 | custom fusion | flops 16384 | bytes 2052 | tf_op jit(solution)/shard_map/scatter-add | solution.py:39
  307.7 79.9 %while.50 = (s32[]{:T(128)}, f32[512,256]{1,0:T(8,128)S(1)}, s32[32,512]{1,0:T(8,128)}, pred[32,512]{1,0:T(8,128)(4,1)S(1)}, s32[32,512]{1,0:T(8,128)}, /*index=...) while((s32[]{:T(128)}, f32[512,256]{1,0:T(8,128)S(1)}, ...), condition=%wide.region_4.5_spmd.clone, body=%wide.region_3.4_spmd.clone.sunk | while | flops 168820736 | bytes 1128617 | solution.py:64
  308.4 1.7 convolution_add_fusion.4
  313.4 1.7 convolution_add_fusion.4
  315.9 1.7 convolution_add_fusion.4
  318.4 1.7 convolution_add_fusion.4
  320.9 1.7 convolution_add_fusion.4
  323.4 1.7 convolution_add_fusion.4
  325.9 1.7 convolution_add_fusion.4
  330.9 1.7 convolution_add_fusion.4
  333.4 1.7 convolution_add_fusion.4
  335.9 1.7 convolution_add_fusion.4
  340.9 1.7 convolution_add_fusion.4
  343.4 1.7 convolution_add_fusion.4
  348.4 1.7 convolution_add_fusion.4
  350.9 1.7 convolution_add_fusion.4
  353.4 1.7 convolution_add_fusion.4
  355.9 1.7 convolution_add_fusion.4
  358.4 1.7 convolution_add_fusion.4
  365.9 1.7 convolution_add_fusion.4
  368.4 1.7 convolution_add_fusion.4
  373.4 1.7 convolution_add_fusion.4
  375.9 1.7 convolution_add_fusion.4
  383.4 1.7 convolution_add_fusion.4
  385.9 1.7 convolution_add_fusion.4
  387.7 2.4 broadcast.21.clone
  390.1 144.5 %while.48 = (s32[]{:T(128)}, f32[32,128,256]{2,1,0:T(8,128)}, s32[32]{0:T(128)S(1)}, s32[32,512]{1,0:T(8,128)}, pred[32,512]{1,0:T(8,128)(4,1)S(1)}, /*index=5*/...) while((s32[]{:T(128)}, f32[32,128,256]{2,1,0:T(8,128)}, ...), condition=%wide.region_6.7_spmd, body=%wide.region_5.6_spmd.sunk | while | flops 168558592 | bytes 408219 | solution.py:82
  534.8 188.5 %reduce-scatter.3.cloned.1.call-done = f32[128,256]{1,0:T(8,128)} async-done(((f32[4096,256]{1,0:T(8,128)}), f32[128,256]{1,0:T(8,128)}) %reduce-scatter.3.cloned.1.call-update) | async-done | bytes 131088 | tf_op jit(solution)/shard_map/reduce_scatter | solution.py:86
  723.3 6.7 all-gather
  730.9 66.2 %all-gather.7.cloned.1.call-done = bf16[4096,256]{1,0:T(8,128)(2,1)} async-done(((bf16[128,256]{1,0:T(8,128)(2,1)}), bf16[4096,256]{1,0:T(8,128)(2,1)}) %all-gather.7.cloned.1.call-update) | async-done | bytes 2097168 | tf_op jit(solution)/shard_map/all_gather | solution.py:105
  797.1 79.9 %while.51 = (s32[]{:T(128)}, f32[512,256]{1,0:T(8,128)S(1)}, s32[32,512]{1,0:T(8,128)}, pred[32,512]{1,0:T(8,128)(4,1)S(1)}, s32[32,512]{1,0:T(8,128)}, /*index=...) while((s32[]{:T(128)}, f32[512,256]{1,0:T(8,128)S(1)}, ...), condition=%wide.region_10.11_spmd.clone, body=%wide.region_9.10_spmd.clone.sunk | while | flops 168820736 | bytes 1128617 | solution.py:64
  805.3 1.7 convolution_add_fusion.5
  807.8 1.7 convolution_add_fusion.5
  822.8 1.7 convolution_add_fusion.5
  825.3 1.7 convolution_add_fusion.5
  840.3 1.7 convolution_add_fusion.5
  842.8 1.7 convolution_add_fusion.5
  857.8 1.7 convolution_add_fusion.5
  860.3 1.7 convolution_add_fusion.5
  875.3 1.7 convolution_add_fusion.5
  877.2 2.4 broadcast.21
  879.6 144.6 %while.49 = (s32[]{:T(128)}, f32[32,128,256]{2,1,0:T(8,128)}, s32[32]{0:T(128)S(1)}, s32[32,512]{1,0:T(8,128)}, pred[32,512]{1,0:T(8,128)(4,1)S(1)}, /*index=5*/...) while((s32[]{:T(128)}, f32[32,128,256]{2,1,0:T(8,128)}, ...), condition=%wide.region_12.13_spmd, body=%wide.region_11.12_spmd.sunk | while | flops 168558592 | bytes 408219 | solution.py:82
  1024.3 190.6 %reduce-scatter.5.cloned.1.call-done = f32[128,256]{1,0:T(8,128)} async-done(((f32[4096,256]{1,0:T(8,128)}), f32[128,256]{1,0:T(8,128)}) %reduce-scatter.5.cloned.1.call-update) | async-done | bytes 131088 | tf_op jit(solution)/shard_map/reduce_scatter | solution.py:86
  1214.9 6.7 all-gather.1
  1224.1 342.4 %all-reduce.2.cloned.1.call-done = f32[256,256]{0,1:T(8,128)} async-done(((f32[256,256]{0,1:T(8,128)}), f32[256,256]{0,1:T(8,128)}) %all-reduce.2.cloned.1.call-update) | async-done | bytes 262160 | tf_op jit(solution)/shard_map/psum | solution.py:117
  1566.4 1.8 copy.11
  (456 shorter events, 277.5 us)
Async XLA Ops:
  7.2 183.8 %copy-start = (bf16[256,256]{1,0:T(8,128)(2,1)S(1)}, bf16[256,256]{1,0:T(8,128)(2,1)}, u32[]{:S(2)}) copy-start(bf16[256,256]{1,0:T(8,128)(2,1)} %param.16) | copy-start | bytes 393220
  7.2 300.5 %all-gather.5.cloned.1.call-start = ((), (), s32[]{:S(2)}) async-start(), calls=%async_computation.2 | async-start | bytes 2162688 | tf_op jit(solution)/shard_map/all_gather | solution.py:95
  192.6 530.7 %reduce-scatter.3.cloned.1.call-start = ((), (), s32[]{:S(2)}) async-start(), calls=%async_computation.3 | async-start | bytes 4325376 | tf_op jit(solution)/shard_map/reduce_scatter | solution.py:86
  534.7 195.3 %copy-start.2 = (bf16[128,256]{1,0:T(8,128)(2,1)S(1)}, bf16[128,256]{1,0:T(8,128)(2,1)}, u32[]{:S(2)}) copy-start(bf16[128,256]{1,0:T(8,128)(2,1)} %param.21) | copy-start | bytes 196612
  534.7 262.3 %all-gather.7.cloned.1.call-start = ((), (), s32[]{:S(2)}) async-start(), calls=%async_computation.4 | async-start | bytes 2162688 | tf_op jit(solution)/shard_map/all_gather | solution.py:105
  730.9 484.0 %reduce-scatter.5.cloned.1.call-start = ((), (), s32[]{:S(2)}) async-start(), calls=%async_computation.5 | async-start | bytes 4325376 | tf_op jit(solution)/shard_map/reduce_scatter | solution.py:86
  1024.2 197.4 %copy-start.1 = (bf16[128,256]{1,0:T(8,128)(2,1)S(1)}, bf16[128,256]{1,0:T(8,128)(2,1)}, u32[]{:S(2)}) copy-start(bf16[128,256]{1,0:T(8,128)(2,1)} %param.15) | copy-start | bytes 196612
  1024.2 542.2 %all-reduce.2.cloned.1.call-start = ((), (), s32[]{:S(2)}) async-start(), calls=%async_computation.6 | async-start | bytes 524288 | tf_op jit(solution)/shard_map/psum | solution.py:117
Sparse Core Ops, SparseCore 0:
  192.7 66.8 all-gather.4
  534.8 188.3 reduce-scatter.2
  731.0 66.0 all-gather.6
  1024.4 190.4 reduce-scatter.4
  1222.7 343.6 all-reduce.1
